TPU v7x, 32 devices: a whole 2x2x4 slice. The times are simulated.
32 devices in a mesh: groups: 2 (over x), tm: 8 (over z, y), tile: 2 (over core).
Axes of the slice: x: 2, y: 2, z: 4, core: 2. Of those that a mesh axis runs over, the one named last changes fastest.
Arguments:
- frames: bfloat16 [2, 16, 2, 64, 2048], P(None, ('groups', 'tm'), 'tile'), parts along dimension 1, may hold values from -6 to 6
- forward_carry: bfloat16 [16, 2, 64, 2048], P(('groups', 'tm'), 'tile'), parts along dimension 0, may hold values from -6 to 6
- backward_carry: bfloat16 [16, 2, 64, 2048], P(('groups', 'tm'), 'tile'), parts along dimension 0, may hold values from -6 to 6
- forward_source: int32 [2, 16, 32], P(None, ('groups', 'tm'), 'tile'), parts along dimension 1, may hold values from 0 to 31, as said below
- backward_source: int32 [2, 16, 32], P(None, ('groups', 'tm'), 'tile'), parts along dimension 1, may hold values from 0 to 31, as said below
- forward_entry: bfloat16 [9, 64, 128], replicated, may hold values from -0.1875 to 0.1875
- forward_blocks: bfloat16 [1, 2, 9, 64, 64], replicated, may hold values from -0.25 to 0.25
- backward_entry: bfloat16 [9, 64, 128], replicated, may hold values from -0.1875 to 0.1875
- backward_blocks: bfloat16 [1, 2, 9, 64, 64], replicated, may hold values from -0.25 to 0.25
- mixing_weight: bfloat16 [64, 128], replicated, may hold values from -0.5 to 0.5
Outputs:
- restored: bfloat16 [2, 16, 2, 64, 2048], P(None, ('groups', 'tm'), 'tile'), parts along dimension 1
- forward_final: bfloat16 [16, 2, 64, 2048], P(('groups', 'tm'), 'tile'), parts along dimension 0
- backward_final: bfloat16 [16, 2, 64, 2048], P(('groups', 'tm'), 'tile'), parts along dimension 0
There are 2 independent parts, one for each index of `groups`. A program takes and returns all parts, laid end to end along the dimension named above; an argument that names none is the same for every part. Nothing has to cross between parts.
Inputs may be any that keep to these rules, and one draw needn't show every extreme that they name: `forward_source`: for each step, segment and destination block of a frame, the block whose forward features it takes: the destination moved by at most one block row and three block columns, kept inside the frame. `backward_source`: the same for backward features.
All inputs are finite; a program needn't handle non-finite values.
Results may differ from a plain program's by a relative error of at most 0.012.
Values may be sent and summed in bfloat16 or wider, within the bound.
A program may use at most 64 MiB of HBM per device.

v0:
```python
import functools

import jax
import jax.numpy as jnp
from jax import lax
from jax.experimental import pallas as pl
from jax.experimental.pallas import tpu as pltpu
from jax.sharding import PartitionSpec as P

RH = 32
RW = 64
BH = 8
BW = 16
LANES = 128
TILES = RH * RW // LANES
GROUP = 4
PACK = 16
CHUNKS = 2
MESH = pl.DeviceIdType.MESH
F32 = jnp.float32
BF16 = jnp.bfloat16


def lrelu(value):
    return jnp.maximum(value, 0.1 * value)


def stacked(piece):
    return jnp.concatenate(
        [jnp.concatenate([piece(3 * a + b) for a in range(3)], axis=1) for b in range(3)], axis=0
    )


def lane_of(rows):
    return lax.broadcasted_iota(jnp.int32, (rows, LANES), 1)


def convolve(source, weight, finish):
    channels = source.shape[0]
    lane = lane_of(channels)
    first_half = lane < RW
    column = lane % RW
    outs = weight.shape[0] // (3 * channels)

    def step(group, _):
        start = pl.multiple_of(group * (GROUP * LANES), GROUP * LANES)
        window = source[:, pl.ds(start, (GROUP + 2) * LANES)]
        tiles = [window[:, t * LANES:(t + 1) * LANES] for t in range(GROUP + 2)]
        turned = [pltpu.roll(tile, RW, 1) for tile in tiles]
        between = [jnp.where(first_half, turned[t], turned[t + 1]) for t in range(GROUP + 1)]
        rhs = jnp.concatenate(
            [
                jnp.concatenate(between[:-1], axis=1),
                jnp.concatenate(tiles[1:-1], axis=1),
                jnp.concatenate(between[1:], axis=1),
            ],
            axis=0,
        )
        product = jnp.dot(weight[...], rhs, preferred_element_type=F32)
        for t in range(GROUP):
            sums = []
            for o in range(outs):
                left, mid, right = (
                    product[(3 * o + b) * channels:(3 * o + b + 1) * channels, t * LANES:(t + 1) * LANES]
                    for b in range(3)
                )
                left = jnp.where(column == 0, 0.0, pltpu.roll(left, 1, 1))
                right = jnp.where(column == RW - 1, 0.0, pltpu.roll(right, LANES - 1, 1))
                sums.append(mid + left + right)
            finish(group * GROUP + t, sums)
        return _

    lax.fori_loop(0, TILES // GROUP, step, 0)


def at_tile(tile, padded):
    return pl.ds(pl.multiple_of((tile + padded) * LANES, LANES), LANES)


def turned_columns(tile, steps, lane):
    if steps == 0:
        return tile
    shift = steps * BW
    inside = pltpu.roll(tile, shift, 1)
    wrapped = pltpu.roll(tile, (shift - RW) % LANES, 1)
    return jnp.where(lane % RW >= shift, inside, wrapped)


def by_column(block_of_lane, values):
    spread = jnp.full(block_of_lane.shape, values[0], jnp.int32)
    for q in range(1, len(values)):
        spread = jnp.where(block_of_lane == q, values[q], spread)
    return spread


def warp(arrived, sources, moment, target):
    channels = target.shape[0]
    cols = RW // BW
    rows = RH // BH
    tiles_of_block = BH * RW // LANES
    lane = lane_of(PACK)
    block_of_lane = lane % RW // BW

    def step(row, _):
        regions, moves, turns = [], [], []
        for col in range(cols):
            block = sources[moment, row * cols + col]
            within = lax.rem(block, rows * cols)
            regions.append(lax.div(block, rows * cols))
            moves.append(lax.div(within, cols) - row)
            turns.append(lax.rem(col - lax.rem(within, cols) + cols, cols))
        turn = by_column(block_of_lane, turns)
        picks = []
        for steps in range(cols):
            order = [(q + steps) % cols for q in range(cols)]
            region = by_column(block_of_lane, [regions[c] for c in order])
            move = by_column(block_of_lane, [moves[c] for c in order])
            picks.append((region == 1, move < 0, move > 0, turn == steps))
        near = (jnp.maximum(row - 1, 0), row, jnp.minimum(row + 1, rows - 1))
        for t in range(tiles_of_block):
            for part in range(channels // PACK):
                held = pl.ds(part * PACK, PACK)
                tiles = [
                    [arrived[region, held, at_tile(near_row * tiles_of_block + t, 0)] for region in range(2)]
                    for near_row in near
                ]
                result = None
                for steps in range(cols):
                    second, above, below, wanted = picks[steps]
                    up, same, down = (jnp.where(second, pair[1], pair[0]) for pair in tiles)
                    moved = jnp.where(above, up, jnp.where(below, down, same))
                    moved = turned_columns(moved, steps, lane)
                    result = moved if result is None else jnp.where(wanted, moved, result)
                target[held, at_tile(row * tiles_of_block + t, 1)] = result
        return _

    lax.fori_loop(0, rows, step, 0)


def kernel(
    count,
    frames,
    carry_f,
    carry_b,
    src_f,
    src_b,
    entry_f,
    blocks_f,
    entry_b,
    blocks_b,
    mixing,
    restored,
    final_f,
    final_b,
    arrived_0f,
    arrived_0b,
    arrived_1f,
    arrived_1b,
    state,
    padded,
    hidden,
    inner,
    pre,
    frame_w,
    warp_w,
    block_w,
    send_sem,
    recv_sem,
    pass_sem,
    got_sem,
):
    ticks, channels, pixels = frames.shape
    arrived = ((arrived_0f, arrived_0b), (arrived_1f, arrived_1b))
    me = lax.axis_index("tm")
    side = lax.axis_index("tile")
    other = 1 - side
    to = (me + 1, me - 1)
    has_to = (me < count - 1, me > 0)
    has_from = (me > 0, me < count - 1)

    barrier = pltpu.get_barrier_semaphore()
    pl.semaphore_signal(barrier, inc=1, device_id={"tile": other}, device_id_type=MESH)
    for d in range(2):
        @pl.when(has_to[d])
        def _(d=d):
            pl.semaphore_signal(barrier, inc=1, device_id={"tm": to[d]}, device_id_type=MESH)
    pl.semaphore_wait(barrier, 1 + jnp.minimum(me, 1) + jnp.minimum(count - 1 - me, 1))

    part = channels // CHUNKS

    def sending(moment, d, chunk):
        rows = pl.ds(chunk * part, part)
        origin = (carry_f, carry_b)[d].at[rows] if moment == 0 else state.at[d, rows]
        return pltpu.make_async_remote_copy(
            src_ref=origin,
            dst_ref=arrived[moment][d].at[side, rows],
            send_sem=send_sem.at[moment, d, chunk],
            recv_sem=recv_sem.at[moment, d, chunk],
            device_id={"tm": to[d]},
            device_id_type=MESH,
        )

    def passing(moment, d, chunk):
        rows = pl.ds(chunk * part, part)
        return pltpu.make_async_remote_copy(
            src_ref=arrived[moment][d].at[side, rows],
            dst_ref=arrived[moment][d].at[side, rows],
            send_sem=pass_sem.at[moment, d, chunk],
            recv_sem=got_sem.at[moment, d, chunk],
            device_id={"tile": other},
            device_id_type=MESH,
        )

    def send(moment, d):
        @pl.when(has_to[d])
        def _():
            for chunk in range(CHUNKS):
                sending(moment, d, chunk).start()

    def receive(moment, d):
        @pl.when(has_from[d])
        def _():
            for chunk in range(CHUNKS):
                sending(moment, d, chunk).wait_recv()
                passing(moment, d, chunk).start()
            for chunk in range(CHUNKS):
                passing(moment, d, chunk).wait_recv()

    send(0, 0)
    send(0, 1)

    for d in range(2):
        @pl.when(jnp.logical_not(has_from[d]))
        def _(d=d):
            for moment in range(ticks):
                for region in range(2):
                    arrived[moment][d][region] = jnp.zeros((channels, pixels), BF16)
    edge = jnp.zeros((channels, LANES), BF16)
    for buffer in (padded, hidden, inner):
        buffer[:, :LANES] = edge
        buffer[:, (TILES + 1) * LANES:] = edge
    for d, (entry, blocks) in enumerate(((entry_f, blocks_f), (entry_b, blocks_b))):
        frame_w[3 * channels * d:3 * channels * (d + 1)] = stacked(lambda tap: entry[tap, :, :channels])
        warp_w[d] = stacked(lambda tap: entry[tap, :, channels:])
        for j in range(2):
            block_w[d, j] = stacked(lambda tap: blocks[0, j, tap])

    for moment in range(ticks):
        padded[:, LANES:(TILES + 1) * LANES] = frames[moment]

        def keep(tile, sums):
            for d in range(2):
                pre[moment, d, :, at_tile(tile, 0)] = sums[d]

        convolve(padded, frame_w, keep)

    def advance(moment, d):
        receive(moment, d)
        warp(arrived[moment][d], (src_f, src_b)[d], moment, padded)

        def entered(tile, sums):
            value = lrelu(pre[moment, d, :, at_tile(tile, 0)] + sums[0])
            hidden[:, at_tile(tile, 1)] = value.astype(BF16)

        convolve(padded, warp_w.at[d], entered)

        def inside(tile, sums):
            inner[:, at_tile(tile, 1)] = lrelu(sums[0]).astype(BF16)

        convolve(hidden, block_w.at[d, 0], inside)

        def added(tile, sums):
            value = hidden[:, at_tile(tile, 1)].astype(F32) + sums[0]
            if moment < ticks - 1:
                state[d, :, at_tile(tile, 0)] = value.astype(BF16)
            else:
                (final_f, final_b)[d][:, at_tile(tile, 0)] = value.astype(BF16)

        convolve(inner, block_w.at[d, 1], added)

    def restore(moment):
        halves = (state.at[0], state.at[1]) if moment < ticks - 1 else (final_f, final_b)

        def step(group, _):
            lanes = pl.ds(pl.multiple_of(group * (GROUP * LANES), GROUP * LANES), GROUP * LANES)
            both = jnp.concatenate([halves[0][:, lanes], halves[1][:, lanes]], axis=0)
            mixed = jnp.dot(mixing[...], both, preferred_element_type=F32)
            restored[moment, :, lanes] = (frames[moment, :, lanes].astype(F32) + mixed).astype(BF16)
            return _

        lax.fori_loop(0, TILES // GROUP, step, 0)

    for moment in range(ticks):
        for d in range(2):
            advance(moment, d)
            if moment < ticks - 1:
                send(moment + 1, d)
        restore(moment)

    for moment in range(ticks):
        for d in range(2):
            for chunk in range(CHUNKS):
                @pl.when(has_to[d])
                def _():
                    sending(moment, d, chunk).wait_send()

                @pl.when(has_from[d])
                def _():
                    passing(moment, d, chunk).wait_send()


def shards(
    frames,
    forward_carry,
    backward_carry,
    forward_source,
    backward_source,
    forward_entry,
    forward_blocks,
    backward_entry,
    backward_blocks,
    mixing_weight,
):
    ticks, _, _, channels, pixels = frames.shape
    vmem = pl.BlockSpec(memory_space=pltpu.VMEM)
    smem = pl.BlockSpec(memory_space=pltpu.SMEM)
    flat = jax.ShapeDtypeStruct((channels, pixels), BF16)
    wide = pixels + 2 * LANES
    semaphores = pltpu.SemaphoreType.DMA((ticks, 2, CHUNKS))
    restored, final_f, final_b = pl.pallas_call(
        functools.partial(kernel, lax.axis_size("tm")),
        out_shape=(jax.ShapeDtypeStruct((ticks, channels, pixels), BF16), flat, flat),
        in_specs=[vmem] * 3 + [smem] * 2 + [vmem] * 5,
        out_specs=(vmem, vmem, vmem),
        scratch_shapes=[
            *[pltpu.VMEM((2, channels, pixels), BF16)] * (2 * ticks),
            pltpu.VMEM((2, channels, pixels), BF16),
            pltpu.VMEM((channels, wide), BF16),
            pltpu.VMEM((channels, wide), BF16),
            pltpu.VMEM((channels, wide), BF16),
            pltpu.VMEM((ticks, 2, channels, pixels), F32),
            pltpu.VMEM((6 * channels, 3 * channels), BF16),
            pltpu.VMEM((2, 3 * channels, 3 * channels), BF16),
            pltpu.VMEM((2, 2, 3 * channels, 3 * channels), BF16),
            semaphores,
            semaphores,
            semaphores,
            semaphores,
        ],
        compiler_params=pltpu.CompilerParams(collective_id=0, has_side_effects=True),
        name="propagate",
    )(
        frames.reshape(ticks, channels, pixels),
        forward_carry.reshape(channels, pixels),
        backward_carry.reshape(channels, pixels),
        forward_source.reshape(ticks, -1),
        backward_source.reshape(ticks, -1),
        forward_entry,
        forward_blocks,
        backward_entry,
        backward_blocks,
        mixing_weight,
    )
    return restored[:, None, None], final_f[None, None], final_b[None, None]


def solution(mesh):
    placed = (
        P(None, ("groups", "tm"), "tile", None, None),
        P(("groups", "tm"), "tile", None, None),
        P(("groups", "tm"), "tile", None, None),
        P(None, ("groups", "tm"), "tile"),
        P(None, ("groups", "tm"), "tile"),
        P(),
        P(),
        P(),
        P(),
        P(),
    )
    return jax.shard_map(
        shards,
        mesh=mesh,
        in_specs=placed,
        out_specs=(
            P(None, ("groups", "tm"), "tile", None, None),
            P(("groups", "tm"), "tile", None, None),
            P(("groups", "tm"), "tile", None, None),
        ),
        check_vma=False,
    )
```

profile of v0, /device:TPU:1, one launch (start us, length us, event | category | flops | bytes accessed | tf_op | source)
XLA Modules:
  0.0 51.0 jit_solution(7056262382953329910)
XLA Ops:
  0.6 46.7 %propagate.1 = (bf16[2,64,2048]{2,1,0:T(8,128)(2,1)}, bf16[64,2048]{1,0:T(8,128)(2,1)}, bf16[64,2048]{1,0:T(8,128)(2,1)}) custom-call(bf16[2,64,2048]{2,1,0:T(8,128)(2,1)} %bitcast.10, bf16[64,2048]{1,0:T(8,128)(2,1)} %bitcast.12, bf16[64,2048]{1,0:T(8,128)(2,1)} %bitcast.13, s32[2,16]{1,0:T(2,128)} %bitcast.16, s32[2,16]{1,0:T(2,128)} %bitcast.17, ...), custom_call_target="tpu_custom_call" | custom-call | tf_op jit(solution)/shard_map/propagate/pallas_call | solution.py:330
  47.3 0.0 copy-start.1
  47.3 1.9 %copy.17 = bf16[2,1,1,64,2048]{4,3,2,1,0:T(8,128)(2,1)} copy(bf16[2,1,1,64,2048]{4,3,2,1,0:T(8,128)(2,1)} %bitcast.11) | data formatting | bytes 1048576
  49.2 0.0 copy-done.1
  49.2 0.0 copy-start
  49.2 0.7 %copy.18 = bf16[1,1,64,2048]{3,2,1,0:T(8,128)(2,1)} copy(bf16[1,1,64,2048]{3,2,1,0:T(8,128)(2,1)S(1)} %bitcast.15) | data formatting | bytes 524288
  49.9 0.3 copy-done
  50.3 0.7 %copy.19 = bf16[1,1,64,2048]{3,2,1,0:T(8,128)(2,1)} copy(bf16[1,1,64,2048]{3,2,1,0:T(8,128)(2,1)S(1)} %bitcast.14) | data formatting | bytes 524288
Async XLA Ops:
  47.3 1.9 %copy-start.1 = (bf16[64,2048]{1,0:T(8,128)(2,1)S(1)}, bf16[64,2048]{1,0:T(8,128)(2,1)}, u32[]{:S(2)}) copy-start(bf16[64,2048]{1,0:T(8,128)(2,1)} %get-tuple-element.7) | copy-start | bytes 786436
  49.2 1.0 %copy-start = (bf16[64,2048]{1,0:T(8,128)(2,1)S(1)}, bf16[64,2048]{1,0:T(8,128)(2,1)}, u32[]{:S(2)}) copy-start(bf16[64,2048]{1,0:T(8,128)(2,1)} %get-tuple-element.8) | copy-start | bytes 786436
where the time goes:
time: 51.2 us; the launch traced here: 51 us
  Pallas kernels  46.7 us (91%)
  local copies, waits for them, and re-layouts  3.67 us (7%)
  between operations  0.65 us (1%)
    pallas_call x1, Pallas kernels, shards(): pl.pallas_call(functools.partial(kernel, lax.axis_size('tm')), out_shape=...  46.7 us
    unnamed x7, local copies, waits for them, and re-layouts  3.67 us

commit v1 on v0

--- a/solution.py
+++ b/solution.py
@@ -13,7 +13,7 @@
 BW = 16
 LANES = 128
 TILES = RH * RW // LANES
-GROUP = 4
+GROUP = 16
 PACK = 16
 CHUNKS = 2
 MESH = pl.DeviceIdType.MESH
@@ -307,6 +307,21 @@
                 @pl.when(has_from[d])
                 def _():
                     passing(moment, d, chunk).wait_send()
+
+
+def hand_over(*refs):
+    third = len(refs) // 4
+    given, out, held = refs[:third], refs[third:2 * third], refs[2 * third:3 * third]
+    sems = refs[3 * third:]
+    taken = [pltpu.make_async_copy(g, h, s.at[0]) for g, h, s in zip(given, held, sems)]
+    put = [pltpu.make_async_copy(h, o, s.at[1]) for h, o, s in zip(held, out, sems)]
+    for copy in taken:
+        copy.start()
+    for first, second in zip(taken, put):
+        first.wait()
+        second.start()
+    for copy in put:
+        copy.wait()
 
 
 def shards(
@@ -361,6 +376,17 @@
         backward_blocks,
         mixing_weight,
     )
+    results = (restored, final_f, final_b)
+    anywhere = pl.BlockSpec(memory_space=pl.ANY)
+    restored, final_f, final_b = pl.pallas_call(
+        hand_over,
+        out_shape=tuple(jax.ShapeDtypeStruct(r.shape, r.dtype) for r in results),
+        in_specs=[anywhere] * len(results),
+        out_specs=(anywhere,) * len(results),
+        scratch_shapes=[pltpu.VMEM(r.shape, r.dtype) for r in results]
+        + [pltpu.SemaphoreType.DMA((2,))] * len(results),
+        name="hand_over",
+    )(*results)
     return restored[:, None, None], final_f[None, None], final_b[None, None]
 
 

time: 51.2 us -> 41.4 us (0.81)
  the two profiles are of different devices: /device:TPU:1 before, /device:TPU:11 now
where the time goes in v1:
time: 41.4 us; the launch traced here: 41.2 us
  Pallas kernels  40.6 us (98%)
  between operations  0.64 us (2%)
    pallas_call x1, Pallas kernels, shards(): pl.pallas_call(functools.partial(kernel, lax.axis_size('tm')), out_shape=...  38.5 us
    pallas_call x1, Pallas kernels, shards(): pl.pallas_call(hand_over, out_shape=tuple((jax.ShapeDtypeStruct(r.shape,...  2.06 us

profile of v1, /device:TPU:11, one launch (start us, length us, event | category | flops | bytes accessed | tf_op | source)
XLA Modules:
  0.0 41.2 jit_solution(17685127706088194591)
XLA Ops:
  0.6 38.5 %propagate.1 = (bf16[2,64,2048]{2,1,0:T(8,128)(2,1)}, bf16[64,2048]{1,0:T(8,128)(2,1)}, bf16[64,2048]{1,0:T(8,128)(2,1)}) custom-call(bf16[2,64,2048]{2,1,0:T(8,128)(2,1)} %bitcast.10, bf16[64,2048]{1,0:T(8,128)(2,1)} %bitcast.11, bf16[64,2048]{1,0:T(8,128)(2,1)} %bitcast.12, s32[2,16]{1,0:T(2,128)} %bitcast.13, s32[2,16]{1,0:T(2,128)} %bitcast.14, ...), custom_call_target="tpu_custom_call" | custom-call | tf_op jit(solution)/shard_map/propagate/pallas_call | solution.py:345
  39.2 2.1 %hand_over.1 = (bf16[2,64,2048]{2,1,0:T(8,128)(2,1)}, bf16[64,2048]{1,0:T(8,128)(2,1)}, bf16[64,2048]{1,0:T(8,128)(2,1)}) custom-call(bf16[2,64,2048]{2,1,0:T(8,128)(2,1)} %get-tuple-element.9.refs_0_, bf16[64,2048]{1,0:T(8,128)(2,1)} %get-tuple-element.10.refs_1_, bf16[64,2048]{1,0:T(8,128)(2,1)} %get-tuple-element.11.refs_2_), custom_call_target="tpu_custom_call" | custom-call | tf_op jit(solution)/shard_map/hand_over/pallas_call | solution.py:381

commit v2 on v1

--- a/solution.py
+++ b/solution.py
@@ -134,7 +134,7 @@
                 target[held, at_tile(row * tiles_of_block + t, 1)] = result
         return _
 
-    lax.fori_loop(0, rows, step, 0)
+    lax.fori_loop(0, rows, step, 0, unroll=True)
 
 
 def kernel(

time: 41.4 us -> 40.8 us (0.986)
  Pallas kernels: 40.6 us -> 40 us
    pallas_call x1, Pallas kernels: 38.5 us -> 38 us  [shards(): pl.pallas_call(functools.partial(kernel, lax.axis_size('tm')), out_shape=...]
where the time goes in v2:
time: 40.8 us; the launch traced here: 40.7 us
  Pallas kernels  40 us (98%)
  between operations  0.64 us (2%)
    pallas_call x1, Pallas kernels, shards(): pl.pallas_call(functools.partial(kernel, lax.axis_size('tm')), out_shape=...  38 us
    pallas_call x1, Pallas kernels, shards(): pl.pallas_call(hand_over, out_shape=tuple((jax.ShapeDtypeStruct(r.shape,...  2.06 us

profile of v2, /device:TPU:11, one launch (start us, length us, event | category | flops | bytes accessed | tf_op | source)
XLA Modules:
  0.0 40.7 jit_solution(12891622890600677928)
XLA Ops:
  0.6 38.0 %propagate.1 = (bf16[2,64,2048]{2,1,0:T(8,128)(2,1)}, bf16[64,2048]{1,0:T(8,128)(2,1)}, bf16[64,2048]{1,0:T(8,128)(2,1)}) custom-call(bf16[2,64,2048]{2,1,0:T(8,128)(2,1)} %bitcast.10, bf16[64,2048]{1,0:T(8,128)(2,1)} %bitcast.11, bf16[64,2048]{1,0:T(8,128)(2,1)} %bitcast.12, s32[2,16]{1,0:T(2,128)} %bitcast.13, s32[2,16]{1,0:T(2,128)} %bitcast.14, ...), custom_call_target="tpu_custom_call" | custom-call | tf_op jit(solution)/shard_map/propagate/pallas_call | solution.py:345
  38.6 2.1 %hand_over.1 = (bf16[2,64,2048]{2,1,0:T(8,128)(2,1)}, bf16[64,2048]{1,0:T(8,128)(2,1)}, bf16[64,2048]{1,0:T(8,128)(2,1)}) custom-call(bf16[2,64,2048]{2,1,0:T(8,128)(2,1)} %get-tuple-element.9.refs_0_, bf16[64,2048]{1,0:T(8,128)(2,1)} %get-tuple-element.10.refs_1_, bf16[64,2048]{1,0:T(8,128)(2,1)} %get-tuple-element.11.refs_2_), custom_call_target="tpu_custom_call" | custom-call | tf_op jit(solution)/shard_map/hand_over/pallas_call | solution.py:381
